TPU v7x, 32 devices: a whole 2x2x4 slice. The times are simulated.
32 devices in a mesh: ord: 8 (over z, core), gx: 2 (over x), gy: 2 (over y).
Axes of the slice: x: 2, y: 2, z: 4, core: 2. Of those that a mesh axis runs over, the one named last changes fastest.
Arguments:
- distribution: float32 [256, 64, 8, 128], P('ord', 'gx', 'gy'), may hold values from -4.5 to 4.5
- relaxation: float32 [64, 8, 128], P('gx', 'gy'), may hold values from 0.05 to 5
Outputs:
- updated: float32 [256, 64, 8, 128], P('ord', 'gx', 'gy')
- temperature: float32 [64, 8, 128], P('gx', 'gy')
All inputs are finite; a program needn't handle non-finite values.
Results may differ from a plain program's by a relative error of at most 0.0003.
Values sent between devices are 32-bit elements; how exact they have to be, the bound alone decides.
A program may use at most 64 MiB of HBM per device.

v0:
```python
import jax
import jax.numpy as jnp
from jax import lax
from jax.sharding import PartitionSpec as P

NORD = 256
STEPS = 2
SWEEPS = 3
time_step = 0.4
limiter_eps = 0.01
diffusion_mass = 0.5
flux_weight = 2.0
golden_turn = 2.399963229728653


def extended(cells, sides, width):
    for axis, dim in sides:
        count = lax.axis_size(axis)
        ends = count - 1
        head = lax.slice_in_dim(cells, 0, width, axis=dim)
        tail = lax.slice_in_dim(cells, cells.shape[dim] - width, cells.shape[dim], axis=dim)
        cells = jnp.concatenate(
            [
                lax.ppermute(tail, axis, [(i, (i + 1) % count) for i in range(ends)]),
                cells,
                lax.ppermute(head, axis, [((i + 1) % count, i) for i in range(ends)]),
            ],
            axis=dim,
        )
    return cells


def directions(offset, length):
    ordinal = (offset + jnp.arange(length, dtype=jnp.int32)).astype(jnp.float32)
    height = 1.0 - (2.0 * ordinal + 1.0) / NORD
    radius = jnp.sqrt(1.0 - height * height)
    turned = golden_turn * ordinal
    return jnp.stack([radius * jnp.cos(turned), radius * jnp.sin(turned), height])


def window(values, anchor, length, axis_dim):
    return lax.slice_in_dim(values, anchor, anchor + length, axis=axis_dim)


def pad_along(values, width, axis_dim):
    widths = [
        (width, width) if dimension == axis_dim else (0, 0) for dimension in range(values.ndim)
    ]
    return jnp.pad(values, widths)


def source_of(current, local_temp, relax):
    return ((2.0 * relax - time_step) * current + 2.0 * time_step * local_temp) / (
        2.0 * relax + time_step
    )


def axis_flux(padded, temp_pad, relax_pad, along_speed, axis_dim):
    length = padded.shape[axis_dim] - 4
    lower_diff = window(padded, 1, length + 2, axis_dim) - window(padded, 0, length + 2, axis_dim)
    upper_diff = window(padded, 2, length + 2, axis_dim) - window(padded, 1, length + 2, axis_dim)
    centre = window(padded, 1, length + 2, axis_dim)
    slopes = (
        lower_diff * (upper_diff * upper_diff + limiter_eps)
        + upper_diff * (lower_diff * lower_diff + limiter_eps)
    ) / (lower_diff * lower_diff + upper_diff * upper_diff + 2.0 * limiter_eps)
    upwind_low = window(centre, 0, length + 1, axis_dim) + 0.5 * (
        1.0 - time_step * along_speed
    ) * window(slopes, 0, length + 1, axis_dim)
    upwind_high = window(centre, 1, length + 1, axis_dim) - 0.5 * (
        1.0 + time_step * along_speed
    ) * window(slopes, 1, length + 1, axis_dim)
    upwind = jnp.where(along_speed >= 0.0, upwind_low, upwind_high)
    temp_face = 0.5 * (
        window(temp_pad, 0, length + 1, axis_dim) + window(temp_pad, 1, length + 1, axis_dim)
    )
    relax_face = 0.5 * (
        window(relax_pad, 0, length + 1, axis_dim) + window(relax_pad, 1, length + 1, axis_dim)
    )
    edges = (2.0 * relax_face * upwind + 0.5 * time_step * temp_face) / (
        2.0 * relax_face + 0.5 * time_step
    )
    return along_speed * (window(edges, 1, length, axis_dim) - window(edges, 0, length, axis_dim))


def spread(flux_x_pad, flux_y_pad, flux_z):
    flux_z_pad = jnp.pad(flux_z, ((0, 0), (0, 0), (1, 1)))
    result = 0.5 * (flux_x_pad[2:, 1:-1, 1:-1] - flux_x_pad[:-2, 1:-1, 1:-1])
    result = result + 0.5 * (flux_y_pad[1:-1, 2:, 1:-1] - flux_y_pad[1:-1, :-2, 1:-1])
    return result + 0.5 * (flux_z_pad[:, :, 2:] - flux_z_pad[:, :, :-2])


def relax_sweep(potential_pad, driver):
    conduct = 1.0 / (1.0 + potential_pad * potential_pad)
    centre = conduct[1:-1, 1:-1, 1:-1]
    weighted = diffusion_mass * driver
    weights = diffusion_mass + jnp.zeros_like(driver)
    for axis_dim in range(3):
        for anchor in (0, 2):
            picker = tuple(
                (
                    (
                        slice(anchor, anchor + potential_pad.shape[axis_dim] - 2)
                        if dimension == axis_dim
                        else slice(1, -1)
                    )
                    for dimension in range(3)
                )
            )
            couple = 0.5 * (centre + conduct[picker])
            weighted = weighted + couple * potential_pad[picker]
            weights = weights + couple
    return weighted / weights


def transport(current, local_temp, relax, speeds):
    source = source_of(current, local_temp, relax)
    ordinal_rows = source.shape[0]
    stacked = jnp.concatenate([source, local_temp[None], relax[None]], 0)
    widened = extended(stacked, (("gx", 1), ("gy", 2)), 2)
    along_x = widened[:, :, 2:-2, :]
    along_y = widened[:, 2:-2, :, :]
    fluxes = axis_flux(
        along_x[:ordinal_rows],
        along_x[ordinal_rows : ordinal_rows + 1, 1:-1],
        along_x[ordinal_rows + 1 :, 1:-1],
        speeds[0][:, None, None, None],
        1,
    )
    fluxes = fluxes + axis_flux(
        along_y[:ordinal_rows],
        along_y[ordinal_rows : ordinal_rows + 1, :, 1:-1],
        along_y[ordinal_rows + 1 :, :, 1:-1],
        speeds[1][:, None, None, None],
        2,
    )
    fluxes = fluxes + axis_flux(
        pad_along(source, 2, 3),
        pad_along(local_temp[None], 1, 3),
        pad_along(relax[None], 1, 3),
        speeds[2][:, None, None, None],
        3,
    )
    return source - time_step * fluxes


def block_extend(stacked):
    widened = extended(stacked, (("gx", 1), ("gy", 2)), 1)
    return jnp.pad(widened, ((0, 0), (0, 0), (0, 0), (1, 1)))


def diffuse(shares, extend):
    energy = shares[0]
    widened = extend(shares[:3])
    driver = energy - flux_weight * spread(widened[1], widened[2], shares[3])
    potential = relax_sweep(widened[0], driver)
    for rounds in range(1, SWEEPS):
        potential = relax_sweep(extend(potential[None])[0], driver)
    return potential


def local(distribution, relaxation):
    local_count = distribution.shape[0]
    speeds = directions(lax.axis_index("ord") * local_count, local_count)
    current = distribution
    for repeat in range(STEPS):
        local_temp = lax.psum(jnp.sum(current, 0) / NORD, "ord")
        current = transport(current, local_temp, relaxation, speeds)
    partial_value = (
        jnp.concatenate(
            [jnp.sum(current, 0)[None], jnp.sum(speeds[:, :, None, None, None] * current[None], 1)],
            0,
        )
        / NORD
    )
    shares = lax.psum(partial_value, "ord")
    potential = diffuse(shares, block_extend)
    updated = source_of(current, potential, relaxation)
    return (updated, potential)


def solution(mesh):
    placed = (P("ord", "gx", "gy", None), P("gx", "gy", None))
    return jax.shard_map(
        local,
        mesh=mesh,
        in_specs=placed,
        out_specs=(P("ord", "gx", "gy", None), P("gx", "gy", None)),
        check_vma=False,
    )
```

profile of v0, /device:TPU:0, one launch (start us, length us, event | category | flops | bytes accessed | tf_op | source)
XLA Modules:
  0.0 365.7 jit_solution(15019233585724942882)
XLA Ops:
  7.2 2.0 reduce_sum.36
  12.2 56.1 %all-reduce.13.cloned.1.call-done = f32[32,4,128]{2,1,0:T(4,128)} async-done(((f32[32,4,128]{2,1,0:T(4,128)}), f32[32,4,128]{2,1,0:T(4,128)}) %all-reduce.13.cloned.1.call-update) | async-done | bytes 65552 | tf_op jit(solution)/shard_map/psum | solution.py:167
  71.5 2.4 add_divide_fusion.1
  74.3 3.4 collective-permute-start
  79.0 2.6 fusion.4
  81.5 3.0 collective-permute-done.1
  85.2 3.5 collective-permute-start.2
  93.6 21.6 %collective-permute-done.2 = f32[34,36,2,128]{3,1,2,0:T(8,128)S(1)} collective-permute-done((f32[34,36,2,128]{3,1,2,0:T(8,128)S(1)}, f32[34,36,2,128]{3,1,2,0:T(8,128)S(1)}, u32[]{:S(2)}, u32[]{:S(2)}) %collective-permute-start.2) | collective-permute-done | bytes 1253408 | tf_op jit(solution)/shard_map/ppermute | solution.py:24
  115.3 4.2 %collective-permute-done.3 = f32[34,36,2,128]{3,1,2,0:T(8,128)S(1)} collective-permute-done((f32[34,36,2,128]{3,1,2,0:T(8,128)S(1)}, f32[34,36,2,128]{3,1,2,0:T(8,128)S(1)}, u32[]{:S(2)}, u32[]{:S(2)}) %collective-permute-start.3) | collective-permute-done | bytes 1253408 | tf_op jit(solution)/shard_map/ppermute | solution.py:26
  119.5 3.6 fusion.18
  123.1 3.5 add_divide_fusion.3
  131.0 53.0 %all-reduce.15.cloned.1.call-done = f32[32,4,128]{2,1,0:T(4,128)} async-done(((f32[32,4,128]{2,1,0:T(4,128)}), f32[32,4,128]{2,1,0:T(4,128)}) %all-reduce.15.cloned.1.call-update) | async-done | bytes 65552 | tf_op jit(solution)/shard_map/psum | solution.py:167
  187.1 2.4 add_divide_fusion
  189.8 3.4 collective-permute-start.4
  194.8 2.6 fusion.12
  197.4 2.8 collective-permute-done.5
  200.8 3.5 collective-permute-start.6
  209.1 21.8 %collective-permute-done.6 = f32[34,36,2,128]{3,1,2,0:T(8,128)S(1)} collective-permute-done((f32[34,36,2,128]{3,1,2,0:T(8,128)S(1)}, f32[34,36,2,128]{3,1,2,0:T(8,128)S(1)}, u32[]{:S(2)}, u32[]{:S(2)}) %collective-permute-start.6) | collective-permute-done | bytes 1253408 | tf_op jit(solution)/shard_map/ppermute | solution.py:24
  230.9 4.2 %collective-permute-done.7 = f32[34,36,2,128]{3,1,2,0:T(8,128)S(1)} collective-permute-done((f32[34,36,2,128]{3,1,2,0:T(8,128)S(1)}, f32[34,36,2,128]{3,1,2,0:T(8,128)S(1)}, u32[]{:S(2)}, u32[]{:S(2)}) %collective-permute-start.7) | collective-permute-done | bytes 1253408 | tf_op jit(solution)/shard_map/ppermute | solution.py:26
  235.1 3.6 fusion.21
  238.7 3.5 add_divide_fusion.2
  243.9 1.8 fusion.156
  248.7 53.9 %all-reduce.17.cloned.1.call-done = f32[4,32,4,128]{3,2,1,0:T(4,128)} async-done(((f32[4,32,4,128]{3,2,1,0:T(4,128)}), f32[4,32,4,128]{3,2,1,0:T(4,128)}) %all-reduce.17.cloned.1.call-update) | async-done | bytes 262160 | tf_op jit(solution)/shard_map/psum | solution.py:176
  303.2 3.4 collective-permute-start.8
  308.9 3.3 collective-permute-done.9
  312.2 3.4 collective-permute-start.10
  318.0 3.6 collective-permute-done.11
  327.1 4.2 %collective-permute-done.13 = f32[1,1,4,128]{3,2,1,0:T(4,128)S(1)} collective-permute-done((f32[1,1,4,128]{3,2,1,0:T(4,128)S(1)}, f32[1,1,4,128]{3,2,1,0:T(4,128)S(1)}, u32[]{:S(2)}, u32[]{:S(2)}) %collective-permute-start.13) | collective-permute-done | bytes 2080 | tf_op jit(solution)/shard_map/ppermute | solution.py:26
  334.3 4.2 %collective-permute-done.15 = f32[1,34,1,128]{3,2,1,0:T(1,128)S(1)} collective-permute-done((f32[1,34,1,128]{3,2,1,0:T(1,128)S(1)}, f32[1,34,1,128]{3,2,1,0:T(1,128)S(1)}, u32[]{:S(2)}, u32[]{:S(2)}) %collective-permute-start.15) | collective-permute-done | bytes 17440 | tf_op jit(solution)/shard_map/ppermute | solution.py:26
  342.6 4.2 %collective-permute-done.17 = f32[1,1,4,128]{3,2,1,0:T(4,128)S(1)} collective-permute-done((f32[1,1,4,128]{3,2,1,0:T(4,128)S(1)}, f32[1,1,4,128]{3,2,1,0:T(4,128)S(1)}, u32[]{:S(2)}, u32[]{:S(2)}) %collective-permute-start.17) | collective-permute-done | bytes 2080 | tf_op jit(solution)/shard_map/ppermute | solution.py:26
  349.8 4.2 %collective-permute-done.19 = f32[1,34,1,128]{3,2,1,0:T(1,128)S(1)} collective-permute-done((f32[1,34,1,128]{3,2,1,0:T(1,128)S(1)}, f32[1,34,1,128]{3,2,1,0:T(1,128)S(1)}, u32[]{:S(2)}, u32[]{:S(2)}) %collective-permute-start.19) | collective-permute-done | bytes 17440 | tf_op jit(solution)/shard_map/ppermute | solution.py:26
  356.1 3.1 copy.53
  (110 shorter events, 55.5 us)
Async XLA Ops:
  7.2 63.9 %copy-start = (f32[32,32,4,128]{3,2,1,0:T(4,128)S(1)}, f32[32,32,4,128]{3,2,1,0:T(4,128)}, u32[]{:S(2)}) copy-start(f32[32,32,4,128]{3,2,1,0:T(4,128)} %param.2) | copy-start | bytes 6291460
  7.2 61.1 %all-reduce.13.cloned.1.call-start = ((), (), s32[]{:S(2)}) async-start(), calls=%async_computation | async-start | bytes 131072 | tf_op jit(solution)/shard_map/psum | solution.py:167
  9.9 174.1 %all-reduce.15.cloned.1.call-start = ((), (), s32[]{:S(2)}) async-start(), calls=%async_computation.1 | async-start | bytes 131072 | tf_op jit(solution)/shard_map/psum | solution.py:167
  74.3 7.3 %collective-permute-start = (f32[34,2,4,128]{3,1,2,0:T(2,128)S(1)}, f32[34,2,4,128]{3,1,2,0:T(2,128)S(1)}, u32[]{:S(2)}, u32[]{:S(2)}) collective-permute-start(f32[34,2,4,128]{3,1,2,0:T(2,128)S(1)} %get-tuple-element.44), channel_id=1, source_target_pairs={{0,2},{1,3},{4,6},{5,7},{8,10},{9,11},{12,14},{13,15},{16,18},{17,... | collective-permute-start | bytes 417800 | tf_op jit(solution)/shard_map/ppermute | solution.py:24
  77.6 6.9 %collective-permute-start.1 = (f32[34,2,4,128]{3,1,2,0:T(2,128)S(1)}, f32[34,2,4,128]{3,1,2,0:T(2,128)S(1)}, u32[]{:S(2)}, u32[]{:S(2)}) collective-permute-start(f32[34,2,4,128]{3,1,2,0:T(2,128)S(1)} %get-tuple-element.45), channel_id=1, source_target_pairs={{2,0},{3,1},{6,4},{7,5},{10,8},{11,9},{14,12},{15,13},{18,16},{19,... | collective-permute-start | bytes 417800 | tf_op jit(solution)/shard_map/ppermute | solution.py:26
  85.2 30.0 %collective-permute-start.2 = (f32[34,36,2,128]{3,1,2,0:T(8,128)S(1)}, f32[34,36,2,128]{3,1,2,0:T(8,128)S(1)}, u32[]{:S(2)}, u32[]{:S(2)}) collective-permute-start(f32[34,36,2,128]{3,1,2,0:T(8,128)S(1)} %get-tuple-element.33), channel_id=1, source_target_pairs={{0,1},{2,3},{4,5},{6,7},{8,9},{10,11},{12,13},{14,15},{16,17},{18,... | collective-permute-start | bytes 3760136 | tf_op jit(solution)/shard_map/ppermute | solution.py:24
  88.7 30.7 %collective-permute-start.3 = (f32[34,36,2,128]{3,1,2,0:T(8,128)S(1)}, f32[34,36,2,128]{3,1,2,0:T(8,128)S(1)}, u32[]{:S(2)}, u32[]{:S(2)}) collective-permute-start(f32[34,36,2,128]{3,1,2,0:T(8,128)S(1)} %get-tuple-element.32), channel_id=1, source_target_pairs={{1,0},{3,2},{5,4},{7,6},{9,8},{11,10},{13,12},{15,14},{17,16},{19,... | collective-permute-start | bytes 3760136 | tf_op jit(solution)/shard_map/ppermute | solution.py:26
  126.6 1.8 copy-start.1
  130.9 171.6 %all-reduce.17.cloned.1.call-start = ((), (), s32[]{:S(2)}) async-start(), calls=%async_computation.2 | async-start | bytes 524288 | tf_op jit(solution)/shard_map/psum | solution.py:176
  189.8 7.5 %collective-permute-start.4 = (f32[34,2,4,128]{3,1,2,0:T(2,128)S(1)}, f32[34,2,4,128]{3,1,2,0:T(2,128)S(1)}, u32[]{:S(2)}, u32[]{:S(2)}) collective-permute-start(f32[34,2,4,128]{3,1,2,0:T(2,128)S(1)} %get-tuple-element.40), channel_id=1, source_target_pairs={{0,2},{1,3},{4,6},{5,7},{8,10},{9,11},{12,14},{13,15},{16,18},{17,... | collective-permute-start | bytes 417800 | tf_op jit(solution)/shard_map/ppermute | solution.py:24
  193.2 6.9 %collective-permute-start.5 = (f32[34,2,4,128]{3,1,2,0:T(2,128)S(1)}, f32[34,2,4,128]{3,1,2,0:T(2,128)S(1)}, u32[]{:S(2)}, u32[]{:S(2)}) collective-permute-start(f32[34,2,4,128]{3,1,2,0:T(2,128)S(1)} %get-tuple-element.41), channel_id=1, source_target_pairs={{2,0},{3,1},{6,4},{7,5},{10,8},{11,9},{14,12},{15,13},{18,16},{19,... | collective-permute-start | bytes 417800 | tf_op jit(solution)/shard_map/ppermute | solution.py:26
  200.8 30.0 %collective-permute-start.6 = (f32[34,36,2,128]{3,1,2,0:T(8,128)S(1)}, f32[34,36,2,128]{3,1,2,0:T(8,128)S(1)}, u32[]{:S(2)}, u32[]{:S(2)}) collective-permute-start(f32[34,36,2,128]{3,1,2,0:T(8,128)S(1)} %get-tuple-element.31), channel_id=1, source_target_pairs={{0,1},{2,3},{4,5},{6,7},{8,9},{10,11},{12,13},{14,15},{16,17},{18,... | collective-permute-start | bytes 3760136 | tf_op jit(solution)/shard_map/ppermute | solution.py:24
  204.3 30.7 %collective-permute-start.7 = (f32[34,36,2,128]{3,1,2,0:T(8,128)S(1)}, f32[34,36,2,128]{3,1,2,0:T(8,128)S(1)}, u32[]{:S(2)}, u32[]{:S(2)}) collective-permute-start(f32[34,36,2,128]{3,1,2,0:T(8,128)S(1)} %get-tuple-element.30), channel_id=1, source_target_pairs={{1,0},{3,2},{5,4},{7,6},{9,8},{11,10},{13,12},{15,14},{17,16},{19,... | collective-permute-start | bytes 3760136 | tf_op jit(solution)/shard_map/ppermute | solution.py:26
  245.8 1.3 copy-start.2
  303.2 5.6 %collective-permute-start.8 = (f32[3,1,4,128]{3,2,1,0:T(4,128)S(1)}, f32[3,1,4,128]{3,2,1,0:T(4,128)S(1)}, u32[]{:S(2)}, u32[]{:S(2)}) collective-permute-start(f32[3,1,4,128]{3,2,1,0:T(4,128)S(1)} %get-tuple-element.49), channel_id=1, source_target_pairs={{0,2},{1,3},{4,6},{5,7},{8,10},{9,11},{12,14},{13,15},{16,18},{17,... | collective-permute-start | bytes 18440 | tf_op jit(solution)/shard_map/ppermute | solution.py:24
  306.6 5.5 %collective-permute-start.9 = (f32[3,1,4,128]{3,2,1,0:T(4,128)S(1)}, f32[3,1,4,128]{3,2,1,0:T(4,128)S(1)}, u32[]{:S(2)}, u32[]{:S(2)}) collective-permute-start(f32[3,1,4,128]{3,2,1,0:T(4,128)S(1)} %get-tuple-element.50), channel_id=1, source_target_pairs={{2,0},{3,1},{6,4},{7,5},{10,8},{11,9},{14,12},{15,13},{18,16},{19,... | collective-permute-start | bytes 18440 | tf_op jit(solution)/shard_map/ppermute | solution.py:26
  312.2 5.8 %collective-permute-start.10 = (f32[3,34,1,128]{3,2,1,0:T(1,128)S(1)}, f32[3,34,1,128]{3,2,1,0:T(1,128)S(1)}, u32[]{:S(2)}, u32[]{:S(2)}) collective-permute-start(f32[3,34,1,128]{3,2,1,0:T(1,128)S(1)} %get-tuple-element.51), channel_id=1, source_target_pairs={{0,1},{2,3},{4,5},{6,7},{8,9},{10,11},{12,13},{14,15},{16,17},{18,... | collective-permute-start | bytes 156680 | tf_op jit(solution)/shard_map/ppermute | solution.py:24
  315.6 6.0 %collective-permute-start.11 = (f32[3,34,1,128]{3,2,1,0:T(1,128)S(1)}, f32[3,34,1,128]{3,2,1,0:T(1,128)S(1)}, u32[]{:S(2)}, u32[]{:S(2)}) collective-permute-start(f32[3,34,1,128]{3,2,1,0:T(1,128)S(1)} %get-tuple-element.52), channel_id=1, source_target_pairs={{1,0},{3,2},{5,4},{7,6},{9,8},{11,10},{13,12},{15,14},{17,16},{19,... | collective-permute-start | bytes 156680 | tf_op jit(solution)/shard_map/ppermute | solution.py:26
  322.5 33.3 %copy-start.3 = (f32[32,32,4,128]{3,1,2,0:T(8,128)S(1)}, f32[32,32,4,128]{3,1,2,0:T(8,128)}, u32[]{:S(2)}) copy-start(f32[32,32,4,128]{3,1,2,0:T(8,128)} %copy-done.2) | copy-start | bytes 6291460
  324.1 3.0 collective-permute-start.12
  325.8 5.5 %collective-permute-start.13 = (f32[1,1,4,128]{3,2,1,0:T(4,128)S(1)}, f32[1,1,4,128]{3,2,1,0:T(4,128)S(1)}, u32[]{:S(2)}, u32[]{:S(2)}) collective-permute-start(f32[1,1,4,128]{3,2,1,0:T(4,128)S(1)} %get-tuple-element.60), channel_id=1, source_target_pairs={{2,0},{3,1},{6,4},{7,5},{10,8},{11,9},{14,12},{15,13},{18,16},{19,... | collective-permute-start | bytes 6152 | tf_op jit(solution)/shard_map/ppermute | solution.py:26
  331.3 3.0 collective-permute-start.14
  332.9 5.6 %collective-permute-start.15 = (f32[1,34,1,128]{3,2,1,0:T(1,128)S(1)}, f32[1,34,1,128]{3,2,1,0:T(1,128)S(1)}, u32[]{:S(2)}, u32[]{:S(2)}) collective-permute-start(f32[1,34,1,128]{3,2,1,0:T(1,128)S(1)} %get-tuple-element.56), channel_id=1, source_target_pairs={{1,0},{3,2},{5,4},{7,6},{9,8},{11,10},{13,12},{15,14},{17,16},{19,... | collective-permute-start | bytes 52232 | tf_op jit(solution)/shard_map/ppermute | solution.py:26
  339.6 3.0 collective-permute-start.16
  341.2 5.5 %collective-permute-start.17 = (f32[1,1,4,128]{3,2,1,0:T(4,128)S(1)}, f32[1,1,4,128]{3,2,1,0:T(4,128)S(1)}, u32[]{:S(2)}, u32[]{:S(2)}) collective-permute-start(f32[1,1,4,128]{3,2,1,0:T(4,128)S(1)} %get-tuple-element.58), channel_id=1, source_target_pairs={{2,0},{3,1},{6,4},{7,5},{10,8},{11,9},{14,12},{15,13},{18,16},{19,... | collective-permute-start | bytes 6152 | tf_op jit(solution)/shard_map/ppermute | solution.py:26
  346.8 3.1 collective-permute-start.18
  348.4 5.6 %collective-permute-start.19 = (f32[1,34,1,128]{3,2,1,0:T(1,128)S(1)}, f32[1,34,1,128]{3,2,1,0:T(1,128)S(1)}, u32[]{:S(2)}, u32[]{:S(2)}) collective-permute-start(f32[1,34,1,128]{3,2,1,0:T(1,128)S(1)} %get-tuple-element.54), channel_id=1, source_target_pairs={{1,0},{3,2},{5,4},{7,6},{9,8},{11,10},{13,12},{15,14},{17,16},{19,... | collective-permute-start | bytes 52232 | tf_op jit(solution)/shard_map/ppermute | solution.py:26
Sparse Core Ops, SparseCore 0:
  10.9 57.4 all-reduce.12
  131.0 52.9 all-reduce.14
  248.8 53.7 all-reduce.16
where the time goes:
time: 367 us; the launch traced here: 366 us
  waiting for transfers between devices  245 us (67%)
  other arithmetic  55.6 us (15%)
  starting transfers between devices  40.7 us (11%)
  between operations  14.5 us (4%)
  local copies, waits for them, and re-layouts  10.4 us (3%)
    psum x2, waiting for transfers between devices, local(): local_temp = lax.psum(jnp.sum(current, 0) / NORD, 'ord')  109 us
    psum x1, waiting for transfers between devices, local(): shares = lax.psum(partial_value, 'ord')  53.9 us
    ppermute x10, waiting for transfers between devices, extended(): lax.ppermute(tail, axis, [(i, (i + 1) % count) for i in range(ends)])  43.7 us
    ppermute x10, waiting for transfers between devices, extended(): lax.ppermute(head, axis, [((i + 1) % count, i) for i in range(ends)])  37.9 us
    ppermute x10, starting transfers between devices, extended(): lax.ppermute(tail, axis, [(i, (i + 1) % count) for i in range(ends)])  27 us
    div x6, other arithmetic, axis_flux(): (lower_diff * (upper_diff * upper_diff + limiter_eps) + upper_diff * (low...  14.3 us
    ppermute x10, starting transfers between devices, extended(): lax.ppermute(head, axis, [((i + 1) % count, i) for i in range(ends)])  13.6 us
    div x6, other arithmetic, axis_flux(): (2.0 * relax_face * upwind + 0.5 * time_step * temp_face) / (2.0 * relax_...  11.4 us
  transfers between devices with their start and end apart: 23, of which 17 were waited for; matrix products, arithmetic and copies ran while one was open for 4% of the time, Pallas kernels for 0%

commit v1 on v0

--- a/solution.py
+++ b/solution.py
@@ -164,7 +164,7 @@
     speeds = directions(lax.axis_index("ord") * local_count, local_count)
     current = distribution
     for repeat in range(STEPS):
-        local_temp = lax.psum(jnp.sum(current, 0) / NORD, "ord")
+        local_temp = jnp.sum(lax.all_gather(jnp.sum(current, 0) / NORD, "ord"), axis=0)
         current = transport(current, local_temp, relaxation, speeds)
     partial_value = (
         jnp.concatenate(

time: 367 us -> 288 us (0.78)
  waiting for transfers between devices: 245 us -> 140 us
  blocking collectives: 0 us -> 31.5 us
    psum x2 -> x0, waiting for transfers between devices: 109 us -> none  [local(): local_temp = lax.psum(jnp.sum(current, 0) / NORD, 'ord')]
    all_gather x0 -> x2, blocking collectives: none -> 31.5 us  [local(): lax.all_gather(jnp.sum(current, 0) / NORD, 'ord')]
    ppermute x10, waiting for transfers between devices: 43.7 us -> 49 us  [extended(): lax.ppermute(tail, axis, [(i, (i + 1) % count) for i in range(ends)])]
  transfers between devices with their start and end apart: 23 -> 21, of which waited for: 17 -> 15; matrix products, arithmetic and copies ran while one was open for 4% -> 6% of each run, Pallas kernels for 0% -> 0%
where the time goes in v1:
time: 288 us; the launch traced here: 287 us
  waiting for transfers between devices  140 us (49%)
  other arithmetic  52.4 us (18%)
  starting transfers between devices  39.5 us (14%)
  blocking collectives  31.5 us (11%)
  between operations  14.8 us (5%)
  local copies, waits for them, and re-layouts  8.67 us (3%)
    psum x1, waiting for transfers between devices, local(): shares = lax.psum(partial_value, 'ord')  54.8 us
    ppermute x10, waiting for transfers between devices, extended(): lax.ppermute(tail, axis, [(i, (i + 1) % count) for i in range(ends)])  49 us
    ppermute x10, waiting for transfers between devices, extended(): lax.ppermute(head, axis, [((i + 1) % count, i) for i in range(ends)])  36.1 us
    all_gather x2, blocking collectives, local(): lax.all_gather(jnp.sum(current, 0) / NORD, 'ord')  31.5 us
    ppermute x10, starting transfers between devices, extended(): lax.ppermute(tail, axis, [(i, (i + 1) % count) for i in range(ends)])  25.8 us
    div x6, other arithmetic, axis_flux(): (lower_diff * (upper_diff * upper_diff + limiter_eps) + upper_diff * (low...  14.3 us
    ppermute x10, starting transfers between devices, extended(): lax.ppermute(head, axis, [((i + 1) % count, i) for i in range(ends)])  13.6 us
    div x6, other arithmetic, axis_flux(): (2.0 * relax_face * upwind + 0.5 * time_step * temp_face) / (2.0 * relax_...  11.4 us
  transfers between devices with their start and end apart: 21, of which 15 were waited for; matrix products, arithmetic and copies ran while one was open for 6% of the time, Pallas kernels for 0%

profile of v1, /device:TPU:0, one launch (start us, length us, event | category | flops | bytes accessed | tf_op | source)
XLA Modules:
  0.0 286.9 jit_solution(14693506546129851804)
XLA Ops:
  9.0 1.9 reduce_sum.58
  10.9 16.5 %all-gather = f32[256,4,128]{2,1,0:T(4,128)S(1)} all-gather(f32[32,4,128]{2,1,0:T(4,128)S(1)} %broadcast_multiply_fusion.3), channel_id=2, replica_groups=mesh['ord'=8,'gx'=2,'gy'=2] {'ord'}, dimensions={0}, use_global_device_ids=true | all-gather | bytes 589824 | tf_op jit(solution)/shard_map/all_gather | solution.py:167
  27.5 2.0 fusion.83
  29.9 3.4 %collective-permute-start = (f32[34,2,4,128]{3,1,2,0:T(2,128)S(1)}, f32[34,2,4,128]{3,1,2,0:T(2,128)S(1)}, u32[]{:S(2)}, u32[]{:S(2)}) collective-permute-start(f32[34,2,4,128]{3,1,2,0:T(2,128)S(1)} %get-tuple-element.44), channel_id=1, source_target_pairs={{0,2},{1,3},{4,6},{5,7},{8,10},{9,11},{12,14},{13,15},{16,18},{17,... | collective-permute-start | bytes 417800 | tf_op jit(solution)/shard_map/ppermute | solution.py:24
  34.9 2.4 add_divide_fusion.1
  37.6 2.5 fusion.4
  41.5 3.5 %collective-permute-start.2 = (f32[34,36,2,128]{3,1,2,0:T(8,128)S(1)}, f32[34,36,2,128]{3,1,2,0:T(8,128)S(1)}, u32[]{:S(2)}, u32[]{:S(2)}) collective-permute-start(f32[34,36,2,128]{3,1,2,0:T(8,128)S(1)} %get-tuple-element.33), channel_id=1, source_target_pairs={{0,1},{2,3},{4,5},{6,7},{8,9},{10,11},{12,13},{14,15},{16,17},{18,... | collective-permute-start | bytes 3760136 | tf_op jit(solution)/shard_map/ppermute | solution.py:24
  49.9 24.3 %collective-permute-done.2 = f32[34,36,2,128]{3,1,2,0:T(8,128)S(1)} collective-permute-done((f32[34,36,2,128]{3,1,2,0:T(8,128)S(1)}, f32[34,36,2,128]{3,1,2,0:T(8,128)S(1)}, u32[]{:S(2)}, u32[]{:S(2)}) %collective-permute-start.2) | collective-permute-done | bytes 1253408 | tf_op jit(solution)/shard_map/ppermute | solution.py:24
  74.3 4.2 %collective-permute-done.3 = f32[34,36,2,128]{3,1,2,0:T(8,128)S(1)} collective-permute-done((f32[34,36,2,128]{3,1,2,0:T(8,128)S(1)}, f32[34,36,2,128]{3,1,2,0:T(8,128)S(1)}, u32[]{:S(2)}, u32[]{:S(2)}) %collective-permute-start.3) | collective-permute-done | bytes 1253408 | tf_op jit(solution)/shard_map/ppermute | solution.py:26
  78.5 3.6 %fusion.18 = (f32[34,36,6,128]{3,1,2,0:T(8,128)S(1)}, f32[34,36,6,128]{3,1,2,0:T(8,128)S(1)}) fusion(f32[1,32,4,128]{3,1,2,0:T(8,128)S(1)} %bitcast.73, f32[34,36,2,128]{3,1,2,0:T(8,128)S(1)} %collective-permute-done.3, f32[34,2,4,128]{3,1,2,0:T(2,128)S(1)} %collective-permute-done.1, f32[1,32,4,128]{3,1,2,0:T(8,128)S(1)} %copy.46, ...), kind=kLoop, calls=%fused_computation.41 | loop fusion | flops 9400320 | bytes 12533760 | tf_op jit(solution)/shard_map/concatenate | solution.py:22
  82.1 3.5 %add_divide_fusion.3 = f32[32,32,6,128]{3,1,2,0:T(8,128)S(1)} fusion(f32[34,36,6,128]{3,1,2,0:T(8,128)S(1)} %get-tuple-element.37, f32[34,36,6,128]{3,1,2,0:T(8,128)S(1)} %get-tuple-element.36, f32[34,36,2,128]{3,1,2,0:T(8,128)S(1)} %collective-permute-done.3, f32[34,2,4,128]{3,1,2,0:T(2,128)S(1)} %collective-permute-done.1, ...), kind=kLoop, calls=%fused_computation.74 | loop fusion | flops 14155776 | bytes 14450688 | tf_op jit(solution)/shard_map/div | solution.py:63
  87.4 1.8 fusion.158
  89.3 15.0 %all-gather.1 = f32[256,4,128]{2,1,0:T(4,128)S(1)} all-gather(f32[32,4,128]{2,1,0:T(4,128)S(1)} %copy_multiply_fusion.1), channel_id=3, replica_groups=mesh['ord'=8,'gx'=2,'gy'=2] {'ord'}, dimensions={0}, use_global_device_ids=true | all-gather | bytes 589824 | tf_op jit(solution)/shard_map/all_gather | solution.py:167
  104.9 2.4 add_divide_fusion
  107.7 4.1 %collective-permute-start.4 = (f32[34,2,4,128]{3,1,2,0:T(2,128)S(1)}, f32[34,2,4,128]{3,1,2,0:T(2,128)S(1)}, u32[]{:S(2)}, u32[]{:S(2)}) collective-permute-start(f32[34,2,4,128]{3,1,2,0:T(2,128)S(1)} %get-tuple-element.40), channel_id=1, source_target_pairs={{0,2},{1,3},{4,6},{5,7},{8,10},{9,11},{12,14},{13,15},{16,18},{17,... | collective-permute-start | bytes 417800 | tf_op jit(solution)/shard_map/ppermute | solution.py:24
  113.4 2.6 fusion.12
  115.9 3.4 %collective-permute-done.5 = f32[34,2,4,128]{3,1,2,0:T(2,128)S(1)} collective-permute-done((f32[34,2,4,128]{3,1,2,0:T(2,128)S(1)}, f32[34,2,4,128]{3,1,2,0:T(2,128)S(1)}, u32[]{:S(2)}, u32[]{:S(2)}) %collective-permute-start.5) | collective-permute-done | bytes 139296 | tf_op jit(solution)/shard_map/ppermute | solution.py:26
  126.3 24.4 %collective-permute-done.6 = f32[34,36,2,128]{3,1,2,0:T(8,128)S(1)} collective-permute-done((f32[34,36,2,128]{3,1,2,0:T(8,128)S(1)}, f32[34,36,2,128]{3,1,2,0:T(8,128)S(1)}, u32[]{:S(2)}, u32[]{:S(2)}) %collective-permute-start.6) | collective-permute-done | bytes 1253408 | tf_op jit(solution)/shard_map/ppermute | solution.py:24
  150.7 4.2 %collective-permute-done.7 = f32[34,36,2,128]{3,1,2,0:T(8,128)S(1)} collective-permute-done((f32[34,36,2,128]{3,1,2,0:T(8,128)S(1)}, f32[34,36,2,128]{3,1,2,0:T(8,128)S(1)}, u32[]{:S(2)}, u32[]{:S(2)}) %collective-permute-start.7) | collective-permute-done | bytes 1253408 | tf_op jit(solution)/shard_map/ppermute | solution.py:26
  154.9 3.6 %fusion.21 = (f32[34,36,6,128]{3,1,2,0:T(8,128)S(1)}, f32[34,36,6,128]{3,1,2,0:T(8,128)S(1)}) fusion(f32[1,32,4,128]{3,1,2,0:T(8,128)S(1)} %bitcast.78, f32[34,36,2,128]{3,1,2,0:T(8,128)S(1)} %collective-permute-done.7, f32[34,2,4,128]{3,1,2,0:T(2,128)S(1)} %collective-permute-done.5, f32[1,32,4,128]{3,1,2,0:T(8,128)S(1)} %copy.50, ...), kind=kLoop, calls=%fused_computation.44 | loop fusion | flops 9400320 | bytes 12533760 | tf_op jit(solution)/shard_map/concatenate | solution.py:22
  158.6 3.5 %add_divide_fusion.2 = f32[32,32,6,128]{3,1,2,0:T(8,128)S(1)} fusion(f32[34,36,6,128]{3,1,2,0:T(8,128)S(1)} %get-tuple-element.35, f32[34,36,6,128]{3,1,2,0:T(8,128)S(1)} %get-tuple-element.34, f32[34,36,2,128]{3,1,2,0:T(8,128)S(1)} %collective-permute-done.7, f32[34,2,4,128]{3,1,2,0:T(2,128)S(1)} %collective-permute-done.5, ...), kind=kLoop, calls=%fused_computation.73 | loop fusion | flops 14155776 | bytes 14450688 | tf_op jit(solution)/shard_map/div | solution.py:63
  163.8 1.9 fusion.156
  168.6 54.8 %all-reduce.11.cloned.1.call-done = f32[4,32,4,128]{3,2,1,0:T(4,128)} async-done(((f32[4,32,4,128]{3,2,1,0:T(4,128)}), f32[4,32,4,128]{3,2,1,0:T(4,128)}) %all-reduce.11.cloned.1.call-update) | async-done | bytes 262160 | tf_op jit(solution)/shard_map/psum | solution.py:176
  224.1 3.4 %collective-permute-start.8 = (f32[3,1,4,128]{3,2,1,0:T(4,128)S(1)}, f32[3,1,4,128]{3,2,1,0:T(4,128)S(1)}, u32[]{:S(2)}, u32[]{:S(2)}) collective-permute-start(f32[3,1,4,128]{3,2,1,0:T(4,128)S(1)} %get-tuple-element.49), channel_id=1, source_target_pairs={{0,2},{1,3},{4,6},{5,7},{8,10},{9,11},{12,14},{13,15},{16,18},{17,... | collective-permute-start | bytes 18440 | tf_op jit(solution)/shard_map/ppermute | solution.py:24
  229.7 3.3 %collective-permute-done.9 = f32[3,1,4,128]{3,2,1,0:T(4,128)S(1)} collective-permute-done((f32[3,1,4,128]{3,2,1,0:T(4,128)S(1)}, f32[3,1,4,128]{3,2,1,0:T(4,128)S(1)}, u32[]{:S(2)}, u32[]{:S(2)}) %collective-permute-start.9) | collective-permute-done | bytes 6176 | tf_op jit(solution)/shard_map/ppermute | solution.py:26
  233.1 3.4 %collective-permute-start.10 = (f32[3,34,1,128]{3,2,1,0:T(1,128)S(1)}, f32[3,34,1,128]{3,2,1,0:T(1,128)S(1)}, u32[]{:S(2)}, u32[]{:S(2)}) collective-permute-start(f32[3,34,1,128]{3,2,1,0:T(1,128)S(1)} %get-tuple-element.51), channel_id=1, source_target_pairs={{0,1},{2,3},{4,5},{6,7},{8,9},{10,11},{12,13},{14,15},{16,17},{18,... | collective-permute-start | bytes 156680 | tf_op jit(solution)/shard_map/ppermute | solution.py:24
  238.9 3.6 %collective-permute-done.11 = f32[3,34,1,128]{3,2,1,0:T(1,128)S(1)} collective-permute-done((f32[3,34,1,128]{3,2,1,0:T(1,128)S(1)}, f32[3,34,1,128]{3,2,1,0:T(1,128)S(1)}, u32[]{:S(2)}, u32[]{:S(2)}) %collective-permute-start.11) | collective-permute-done | bytes 52256 | tf_op jit(solution)/shard_map/ppermute | solution.py:26
  247.9 4.2 %collective-permute-done.13 = f32[1,1,4,128]{3,2,1,0:T(4,128)S(1)} collective-permute-done((f32[1,1,4,128]{3,2,1,0:T(4,128)S(1)}, f32[1,1,4,128]{3,2,1,0:T(4,128)S(1)}, u32[]{:S(2)}, u32[]{:S(2)}) %collective-permute-start.13) | collective-permute-done | bytes 2080 | tf_op jit(solution)/shard_map/ppermute | solution.py:26
  255.2 4.2 %collective-permute-done.15 = f32[1,34,1,128]{3,2,1,0:T(1,128)S(1)} collective-permute-done((f32[1,34,1,128]{3,2,1,0:T(1,128)S(1)}, f32[1,34,1,128]{3,2,1,0:T(1,128)S(1)}, u32[]{:S(2)}, u32[]{:S(2)}) %collective-permute-start.15) | collective-permute-done | bytes 17440 | tf_op jit(solution)/shard_map/ppermute | solution.py:26
  263.4 4.2 %collective-permute-done.17 = f32[1,1,4,128]{3,2,1,0:T(4,128)S(1)} collective-permute-done((f32[1,1,4,128]{3,2,1,0:T(4,128)S(1)}, f32[1,1,4,128]{3,2,1,0:T(4,128)S(1)}, u32[]{:S(2)}, u32[]{:S(2)}) %collective-permute-start.17) | collective-permute-done | bytes 2080 | tf_op jit(solution)/shard_map/ppermute | solution.py:26
  270.7 4.2 %collective-permute-done.19 = f32[1,34,1,128]{3,2,1,0:T(1,128)S(1)} collective-permute-done((f32[1,34,1,128]{3,2,1,0:T(1,128)S(1)}, f32[1,34,1,128]{3,2,1,0:T(1,128)S(1)}, u32[]{:S(2)}, u32[]{:S(2)}) %collective-permute-start.19) | collective-permute-done | bytes 17440 | tf_op jit(solution)/shard_map/ppermute | solution.py:26
  276.9 3.1 %copy.55 = f32[32,32,4,128]{3,2,1,0:T(4,128)} copy(f32[32,32,4,128]{3,1,2,0:T(8,128)S(1)} %add_divide_fusion.6) | data formatting | bytes 4194304
  (106 shorter events, 49.2 us)
Async XLA Ops:
  7.2 216.2 %all-reduce.11.cloned.1.call-start = ((), (), s32[]{:S(2)}) async-start(), calls=%async_computation | async-start | bytes 524288 | tf_op jit(solution)/shard_map/psum | solution.py:176
  29.9 10.2 %collective-permute-start = (f32[34,2,4,128]{3,1,2,0:T(2,128)S(1)}, f32[34,2,4,128]{3,1,2,0:T(2,128)S(1)}, u32[]{:S(2)}, u32[]{:S(2)}) collective-permute-start(f32[34,2,4,128]{3,1,2,0:T(2,128)S(1)} %get-tuple-element.44), channel_id=1, source_target_pairs={{0,2},{1,3},{4,6},{5,7},{8,10},{9,11},{12,14},{13,15},{16,18},{17,... | collective-permute-start | bytes 417800 | tf_op jit(solution)/shard_map/ppermute | solution.py:24
  33.3 7.5 %collective-permute-start.1 = (f32[34,2,4,128]{3,1,2,0:T(2,128)S(1)}, f32[34,2,4,128]{3,1,2,0:T(2,128)S(1)}, u32[]{:S(2)}, u32[]{:S(2)}) collective-permute-start(f32[34,2,4,128]{3,1,2,0:T(2,128)S(1)} %get-tuple-element.45), channel_id=1, source_target_pairs={{2,0},{3,1},{6,4},{7,5},{10,8},{11,9},{14,12},{15,13},{18,16},{19,... | collective-permute-start | bytes 417800 | tf_op jit(solution)/shard_map/ppermute | solution.py:26
  41.5 32.7 %collective-permute-start.2 = (f32[34,36,2,128]{3,1,2,0:T(8,128)S(1)}, f32[34,36,2,128]{3,1,2,0:T(8,128)S(1)}, u32[]{:S(2)}, u32[]{:S(2)}) collective-permute-start(f32[34,36,2,128]{3,1,2,0:T(8,128)S(1)} %get-tuple-element.33), channel_id=1, source_target_pairs={{0,1},{2,3},{4,5},{6,7},{8,9},{10,11},{12,13},{14,15},{16,17},{18,... | collective-permute-start | bytes 3760136 | tf_op jit(solution)/shard_map/ppermute | solution.py:24
  45.0 33.4 %collective-permute-start.3 = (f32[34,36,2,128]{3,1,2,0:T(8,128)S(1)}, f32[34,36,2,128]{3,1,2,0:T(8,128)S(1)}, u32[]{:S(2)}, u32[]{:S(2)}) collective-permute-start(f32[34,36,2,128]{3,1,2,0:T(8,128)S(1)} %get-tuple-element.32), channel_id=1, source_target_pairs={{1,0},{3,2},{5,4},{7,6},{9,8},{11,10},{13,12},{15,14},{17,16},{19,... | collective-permute-start | bytes 3760136 | tf_op jit(solution)/shard_map/ppermute | solution.py:26
  85.6 1.8 copy-start
  107.7 8.2 %collective-permute-start.4 = (f32[34,2,4,128]{3,1,2,0:T(2,128)S(1)}, f32[34,2,4,128]{3,1,2,0:T(2,128)S(1)}, u32[]{:S(2)}, u32[]{:S(2)}) collective-permute-start(f32[34,2,4,128]{3,1,2,0:T(2,128)S(1)} %get-tuple-element.40), channel_id=1, source_target_pairs={{0,2},{1,3},{4,6},{5,7},{8,10},{9,11},{12,14},{13,15},{16,18},{17,... | collective-permute-start | bytes 417800 | tf_op jit(solution)/shard_map/ppermute | solution.py:24
  111.8 7.5 %collective-permute-start.5 = (f32[34,2,4,128]{3,1,2,0:T(2,128)S(1)}, f32[34,2,4,128]{3,1,2,0:T(2,128)S(1)}, u32[]{:S(2)}, u32[]{:S(2)}) collective-permute-start(f32[34,2,4,128]{3,1,2,0:T(2,128)S(1)} %get-tuple-element.41), channel_id=1, source_target_pairs={{2,0},{3,1},{6,4},{7,5},{10,8},{11,9},{14,12},{15,13},{18,16},{19,... | collective-permute-start | bytes 417800 | tf_op jit(solution)/shard_map/ppermute | solution.py:26
  120.0 30.7 %collective-permute-start.6 = (f32[34,36,2,128]{3,1,2,0:T(8,128)S(1)}, f32[34,36,2,128]{3,1,2,0:T(8,128)S(1)}, u32[]{:S(2)}, u32[]{:S(2)}) collective-permute-start(f32[34,36,2,128]{3,1,2,0:T(8,128)S(1)} %get-tuple-element.31), channel_id=1, source_target_pairs={{0,1},{2,3},{4,5},{6,7},{8,9},{10,11},{12,13},{14,15},{16,17},{18,... | collective-permute-start | bytes 3760136 | tf_op jit(solution)/shard_map/ppermute | solution.py:24
  121.6 33.4 %collective-permute-start.7 = (f32[34,36,2,128]{3,1,2,0:T(8,128)S(1)}, f32[34,36,2,128]{3,1,2,0:T(8,128)S(1)}, u32[]{:S(2)}, u32[]{:S(2)}) collective-permute-start(f32[34,36,2,128]{3,1,2,0:T(8,128)S(1)} %get-tuple-element.30), channel_id=1, source_target_pairs={{1,0},{3,2},{5,4},{7,6},{9,8},{11,10},{13,12},{15,14},{17,16},{19,... | collective-permute-start | bytes 3760136 | tf_op jit(solution)/shard_map/ppermute | solution.py:26
  165.7 1.3 copy-start.1
  224.1 5.6 %collective-permute-start.8 = (f32[3,1,4,128]{3,2,1,0:T(4,128)S(1)}, f32[3,1,4,128]{3,2,1,0:T(4,128)S(1)}, u32[]{:S(2)}, u32[]{:S(2)}) collective-permute-start(f32[3,1,4,128]{3,2,1,0:T(4,128)S(1)} %get-tuple-element.49), channel_id=1, source_target_pairs={{0,2},{1,3},{4,6},{5,7},{8,10},{9,11},{12,14},{13,15},{16,18},{17,... | collective-permute-start | bytes 18440 | tf_op jit(solution)/shard_map/ppermute | solution.py:24
  227.5 5.5 %collective-permute-start.9 = (f32[3,1,4,128]{3,2,1,0:T(4,128)S(1)}, f32[3,1,4,128]{3,2,1,0:T(4,128)S(1)}, u32[]{:S(2)}, u32[]{:S(2)}) collective-permute-start(f32[3,1,4,128]{3,2,1,0:T(4,128)S(1)} %get-tuple-element.50), channel_id=1, source_target_pairs={{2,0},{3,1},{6,4},{7,5},{10,8},{11,9},{14,12},{15,13},{18,16},{19,... | collective-permute-start | bytes 18440 | tf_op jit(solution)/shard_map/ppermute | solution.py:26
  233.1 5.8 %collective-permute-start.10 = (f32[3,34,1,128]{3,2,1,0:T(1,128)S(1)}, f32[3,34,1,128]{3,2,1,0:T(1,128)S(1)}, u32[]{:S(2)}, u32[]{:S(2)}) collective-permute-start(f32[3,34,1,128]{3,2,1,0:T(1,128)S(1)} %get-tuple-element.51), channel_id=1, source_target_pairs={{0,1},{2,3},{4,5},{6,7},{8,9},{10,11},{12,13},{14,15},{16,17},{18,... | collective-permute-start | bytes 156680 | tf_op jit(solution)/shard_map/ppermute | solution.py:24
  236.5 6.0 %collective-permute-start.11 = (f32[3,34,1,128]{3,2,1,0:T(1,128)S(1)}, f32[3,34,1,128]{3,2,1,0:T(1,128)S(1)}, u32[]{:S(2)}, u32[]{:S(2)}) collective-permute-start(f32[3,34,1,128]{3,2,1,0:T(1,128)S(1)} %get-tuple-element.52), channel_id=1, source_target_pairs={{1,0},{3,2},{5,4},{7,6},{9,8},{11,10},{13,12},{15,14},{17,16},{19,... | collective-permute-start | bytes 156680 | tf_op jit(solution)/shard_map/ppermute | solution.py:26
  243.3 33.3 %copy-start.2 = (f32[32,32,4,128]{3,1,2,0:T(8,128)S(1)}, f32[32,32,4,128]{3,1,2,0:T(8,128)}, u32[]{:S(2)}) copy-start(f32[32,32,4,128]{3,1,2,0:T(8,128)} %copy-done.1) | copy-start | bytes 6291460
  245.0 3.0 %collective-permute-start.12 = (f32[1,1,4,128]{3,2,1,0:T(4,128)S(1)}, f32[1,1,4,128]{3,2,1,0:T(4,128)S(1)}, u32[]{:S(2)}, u32[]{:S(2)}) collective-permute-start(f32[1,1,4,128]{3,2,1,0:T(4,128)S(1)} %get-tuple-element.59), channel_id=1, source_target_pairs={{0,2},{1,3},{4,6},{5,7},{8,10},{9,11},{12,14},{13,15},{16,18},{17,... | collective-permute-start | bytes 6152 | tf_op jit(solution)/shard_map/ppermute | solution.py:24
  246.6 5.5 %collective-permute-start.13 = (f32[1,1,4,128]{3,2,1,0:T(4,128)S(1)}, f32[1,1,4,128]{3,2,1,0:T(4,128)S(1)}, u32[]{:S(2)}, u32[]{:S(2)}) collective-permute-start(f32[1,1,4,128]{3,2,1,0:T(4,128)S(1)} %get-tuple-element.60), channel_id=1, source_target_pairs={{2,0},{3,1},{6,4},{7,5},{10,8},{11,9},{14,12},{15,13},{18,16},{19,... | collective-permute-start | bytes 6152 | tf_op jit(solution)/shard_map/ppermute | solution.py:26
  252.1 3.0 %collective-permute-start.14 = (f32[1,34,1,128]{3,2,1,0:T(1,128)S(1)}, f32[1,34,1,128]{3,2,1,0:T(1,128)S(1)}, u32[]{:S(2)}, u32[]{:S(2)}) collective-permute-start(f32[1,34,1,128]{3,2,1,0:T(1,128)S(1)} %get-tuple-element.55), channel_id=1, source_target_pairs={{0,1},{2,3},{4,5},{6,7},{8,9},{10,11},{12,13},{14,15},{16,17},{18,... | collective-permute-start | bytes 52232 | tf_op jit(solution)/shard_map/ppermute | solution.py:24
  253.7 5.6 %collective-permute-start.15 = (f32[1,34,1,128]{3,2,1,0:T(1,128)S(1)}, f32[1,34,1,128]{3,2,1,0:T(1,128)S(1)}, u32[]{:S(2)}, u32[]{:S(2)}) collective-permute-start(f32[1,34,1,128]{3,2,1,0:T(1,128)S(1)} %get-tuple-element.56), channel_id=1, source_target_pairs={{1,0},{3,2},{5,4},{7,6},{9,8},{11,10},{13,12},{15,14},{17,16},{19,... | collective-permute-start | bytes 52232 | tf_op jit(solution)/shard_map/ppermute | solution.py:26
  260.4 3.0 %collective-permute-start.16 = (f32[1,1,4,128]{3,2,1,0:T(4,128)S(1)}, f32[1,1,4,128]{3,2,1,0:T(4,128)S(1)}, u32[]{:S(2)}, u32[]{:S(2)}) collective-permute-start(f32[1,1,4,128]{3,2,1,0:T(4,128)S(1)} %get-tuple-element.57), channel_id=1, source_target_pairs={{0,2},{1,3},{4,6},{5,7},{8,10},{9,11},{12,14},{13,15},{16,18},{17,... | collective-permute-start | bytes 6152 | tf_op jit(solution)/shard_map/ppermute | solution.py:24
  262.1 5.5 %collective-permute-start.17 = (f32[1,1,4,128]{3,2,1,0:T(4,128)S(1)}, f32[1,1,4,128]{3,2,1,0:T(4,128)S(1)}, u32[]{:S(2)}, u32[]{:S(2)}) collective-permute-start(f32[1,1,4,128]{3,2,1,0:T(4,128)S(1)} %get-tuple-element.58), channel_id=1, source_target_pairs={{2,0},{3,1},{6,4},{7,5},{10,8},{11,9},{14,12},{15,13},{18,16},{19,... | collective-permute-start | bytes 6152 | tf_op jit(solution)/shard_map/ppermute | solution.py:26
  267.6 3.1 %collective-permute-start.18 = (f32[1,34,1,128]{3,2,1,0:T(1,128)S(1)}, f32[1,34,1,128]{3,2,1,0:T(1,128)S(1)}, u32[]{:S(2)}, u32[]{:S(2)}) collective-permute-start(f32[1,34,1,128]{3,2,1,0:T(1,128)S(1)} %get-tuple-element.53), channel_id=1, source_target_pairs={{0,1},{2,3},{4,5},{6,7},{8,9},{10,11},{12,13},{14,15},{16,17},{18,... | collective-permute-start | bytes 52232 | tf_op jit(solution)/shard_map/ppermute | solution.py:24
  269.2 5.6 %collective-permute-start.19 = (f32[1,34,1,128]{3,2,1,0:T(1,128)S(1)}, f32[1,34,1,128]{3,2,1,0:T(1,128)S(1)}, u32[]{:S(2)}, u32[]{:S(2)}) collective-permute-start(f32[1,34,1,128]{3,2,1,0:T(1,128)S(1)} %get-tuple-element.54), channel_id=1, source_target_pairs={{1,0},{3,2},{5,4},{7,6},{9,8},{11,10},{13,12},{15,14},{17,16},{19,... | collective-permute-start | bytes 52232 | tf_op jit(solution)/shard_map/ppermute | solution.py:26
Sparse Core Ops, SparseCore 0:
  168.7 54.6 all-reduce.10
